TPU v7x, 512 devices: a whole 4x4x16 slice. The times are simulated.
512 devices in a mesh: stn: 64 (over x, z), tm: 8 (over y, core).
Axes of the slice: x: 4, y: 4, z: 16, core: 2. Of those that a mesh axis runs over, the one named last changes fastest.
Arguments:
- right_sides: bfloat16 [2048, 131072], P('tm', 'stn'), may hold values from -6 to 6
- factor_cols: bfloat16 [131072, 512], P('stn'), may hold values from -0.25 to 0.25
- diag_inverses: float32 [2, 256, 256], replicated, as said below
- panel_block: int32 [1], replicated, may hold values from 0 to 510
- decay_rate: float32 [131072], P('stn'), may hold values from 0.00048828125 to 0.1
- gaps: int32 [2048], replicated, may hold values 0 or 1
Outputs:
- filtered: bfloat16 [2048, 131072], P('tm', 'stn')
Inputs may be any that keep to these rules, and one draw needn't show every extreme that they name: `diag_inverses`: each block is lower triangular with diagonal entries between 1 and 2. The two panels are rows 256 * panel_block to 256 * panel_block + 2 * 256 - 1.
All inputs are finite; a program needn't handle non-finite values.
Results may differ from a plain program's by a relative error of at most 0.001.
Values may be sent and summed in bfloat16 or wider, within the bound.
A program may use at most 64 MiB of HBM per device.

v0:
```python
import jax
import jax.numpy as jnp
from jax import lax
from jax.sharding import PartitionSpec as P


def broadcast(block, axis, source):
    block = jnp.where(lax.axis_index(axis) == source, block, jnp.zeros_like(block))
    return lax.psum(block, axis)


def compose(earlier, later):
    new_aa = later[0] * earlier[0] + later[1] * earlier[2]
    new_ab = later[0] * earlier[1] + later[1] * earlier[3]
    new_ba = later[2] * earlier[0] + later[3] * earlier[2]
    new_bb = later[2] * earlier[1] + later[3] * earlier[3]
    new_lv = later[0] * earlier[4] + later[1] * earlier[5] + later[4]
    new_sl = later[2] * earlier[4] + later[3] * earlier[5] + later[5]
    return (new_aa, new_ab, new_ba, new_bb, new_lv, new_sl)


def block_prefix(inputs, gap_flags, rate):
    decay = jnp.exp(-rate)
    gain = 2.0 * rate * jnp.sqrt(rate)
    factor = jnp.where(gap_flags == 1, 0.5, 1.0).astype(jnp.float32)[:, None]
    elements = (
        factor * (decay * (1.0 + rate)),
        factor * decay + 0.0 * inputs,
        factor * (-decay * rate * rate) + 0.0 * inputs,
        factor * (decay * (1.0 - rate)) + 0.0 * inputs,
        jnp.zeros_like(inputs),
        gain * inputs,
    )
    elements = (elements[0] + 0.0 * inputs,) + elements[1:]
    return lax.associative_scan(compose, elements, axis=0)


def solve_panel(block, inverse):
    return lax.dot_general(
        block,
        inverse,
        (((1,), (1,)), ((), ())),
        precision=lax.Precision.HIGHEST,
        preferred_element_type=jnp.float32,
    )


def trailing(work, solved, which, first_row, factor_cols, global_rows):
    panel_rows = solved.shape[1]
    below = (global_rows >= first_row + panel_rows).astype(jnp.float32)
    columns = (
        factor_cols[:, which * panel_rows : (which + 1) * panel_rows].astype(jnp.float32)
        * below[:, None]
    )
    return work - lax.dot_general(
        solved,
        columns,
        (((1,), (1,)), ((), ())),
        precision=lax.Precision.HIGHEST,
        preferred_element_type=jnp.float32,
    )


def place(work, solved, first_row, device_idx):
    stn_rows = work.shape[1]
    holder = first_row // stn_rows
    offset = first_row - holder * stn_rows
    placed = lax.dynamic_update_slice_in_dim(work, solved, offset, 1)
    return jnp.where(device_idx == holder, placed, work)


def panel_step(work, which, start_row, factor_cols, diag_inverses, global_rows, device_idx):
    panel_rows = diag_inverses.shape[1]
    stn_rows = work.shape[1]
    first_row = start_row + which * panel_rows
    holder = first_row // stn_rows
    offset = first_row - holder * stn_rows
    rhs_block = lax.dynamic_slice_in_dim(work, offset, panel_rows, 1)
    solved_here = solve_panel(rhs_block, diag_inverses[which])
    solved = broadcast(solved_here, "stn", holder)
    work = place(work, solved, first_row, device_idx)
    return trailing(work, solved, which, first_row, factor_cols, global_rows)


def on_device(right_sides, factor_cols, diag_inverses, panel_block, decay_rate, gaps):
    work = right_sides.astype(jnp.float32)
    time_rows, stn_rows = work.shape
    panel_rows = diag_inverses.shape[1]
    device_idx = lax.axis_index("stn")
    global_rows = device_idx * stn_rows + lax.iota(jnp.int32, stn_rows)
    start_row = panel_block[0] * panel_rows
    for which in range(2):
        work = panel_step(
            work, which, start_row, factor_cols, diag_inverses, global_rows, device_idx
        )
    time_idx = lax.axis_index("tm")
    groups = lax.axis_size("tm")
    narrow = stn_rows // groups
    series = lax.all_to_all(work, "tm", split_axis=1, concat_axis=0, tiled=True)
    rates = lax.dynamic_slice_in_dim(decay_rate, time_idx * narrow, narrow)
    series_blocks = series.reshape(groups, time_rows, narrow)
    gap_blocks = gaps.reshape(groups, time_rows)

    def advance(carried, element):
        inputs, gap_flags = element
        prefix = block_prefix(inputs, gap_flags, rates)
        level = prefix[0] * carried[0] + prefix[1] * carried[1] + prefix[4]
        slope = prefix[2] * carried[0] + prefix[3] * carried[1] + prefix[5]
        return ((level[-1], slope[-1]), level.astype(jnp.bfloat16))

    zeros_row = jnp.zeros((narrow,), jnp.float32)
    _, levels = lax.scan(advance, (zeros_row, zeros_row), (series_blocks, gap_blocks))
    levels = levels.reshape(groups * time_rows, narrow)
    return lax.all_to_all(levels, "tm", split_axis=0, concat_axis=1, tiled=True)


def solution(mesh):
    return jax.shard_map(
        on_device,
        mesh=mesh,
        in_specs=(P("tm", "stn"), P("stn", None), P(), P(), P("stn"), P()),
        out_specs=P("tm", "stn"),
        check_vma=False,
    )
```

profile of v0, /device:TPU:1, one launch (start us, length us, event | category | flops | bytes accessed | tf_op | source)
XLA Modules:
  0.0 694.7 jit_solution(8325721366704118853)
XLA Ops:
  7.2 2.1 convolution_select_fusion.1
  9.4 2.8 convert_element_type.29
  12.2 260.4 %all-reduce.100.cloned.1.call-done = f32[256,256]{1,0:T(8,128)} async-done(((f32[256,256]{1,0:T(8,128)}), f32[256,256]{1,0:T(8,128)}) %all-reduce.100.cloned.1.call-update) | async-done | bytes 262160 | tf_op jit(solution)/shard_map/psum | solution.py:9
  272.7 1.7 select_dynamic-update-slice_fusion.1
  274.4 4.1 convolution_subtract_fusion.1
  278.5 1.1 convolution_select_fusion
  279.7 261.0 %all-reduce.102.cloned.1.call-done = f32[256,256]{1,0:T(8,128)} async-done(((f32[256,256]{1,0:T(8,128)}), f32[256,256]{1,0:T(8,128)}) %all-reduce.102.cloned.1.call-update) | async-done | bytes 262160 | tf_op jit(solution)/shard_map/psum | solution.py:9
  540.7 3.4 convolution_subtract_fusion
  544.2 1.5 copy.12
  545.7 15.1 %all-to-all-start = ((f32[256,8,256]{2,0,1:T(8,128)}), f32[256,8,256]{2,0,1:T(8,128)}, u32[]{:S(2)}, u32[]{:S(2)}) async-start(f32[256,8,256]{2,0,1:T(8,128)} %bitcast.38), calls=%async_computation | async-start | bytes 4194304 | tf_op jit(solution)/shard_map/all_to_all | solution.py:99
  560.8 0.8 fusion.26
  561.5 25.5 %all-to-all-done = f32[256,8,256]{2,0,1:T(8,128)} async-done(((f32[256,8,256]{2,0,1:T(8,128)}), f32[256,8,256]{2,0,1:T(8,128)}, u32[]{:S(2)}, u32[]{:S(2)}) %all-to-all-start) | async-done | bytes 2097184 | tf_op jit(solution)/shard_map/all_to_all | solution.py:99
  587.1 80.3 %while.17 = (s32[]{:T(128)}, f32[256]{0:T(256)S(1)}, f32[256]{0:T(256)S(1)}, bf16[8,256,256]{2,1,0:T(8,128)(2,1)}, s32[8,256]{1,0:T(8,128)S(1)}, /*index=5*/f32[...) while((s32[]{:T(128)}, f32[256]{0:T(256)S(1)}, ...), condition=%wide.region_3.4_spmd, body=%wide.region_2.3_spmd.sunk | while | flops 4393474 | bytes 37127632 | solution.py:112
  587.1 1.1 multiply_add_fusion.88
  589.2 0.2 slice.2362
  589.7 0.2 slice.2363
  595.6 0.1 multiply_add_fusion.109
  596.2 0.8 bitcast_dynamic-update-slice_fusion.2
  597.1 1.1 multiply_add_fusion.88
  599.2 0.2 slice.2362
  599.8 0.2 slice.2363
  606.3 0.8 bitcast_dynamic-update-slice_fusion.2
  607.2 1.1 multiply_add_fusion.88
  609.2 0.2 slice.2362
  609.8 0.2 slice.2363
  616.3 0.8 bitcast_dynamic-update-slice_fusion.2
  617.2 1.1 multiply_add_fusion.88
  619.3 0.2 slice.2362
  619.8 0.2 slice.2363
  626.4 0.8 bitcast_dynamic-update-slice_fusion.2
  627.2 1.1 multiply_add_fusion.88
  629.3 0.2 slice.2362
  629.9 0.2 slice.2363
  636.4 0.8 bitcast_dynamic-update-slice_fusion.2
  637.3 1.1 multiply_add_fusion.88
  639.3 0.2 slice.2362
  639.9 0.2 slice.2363
  646.4 0.8 bitcast_dynamic-update-slice_fusion.2
  647.3 1.1 multiply_add_fusion.88
  649.4 0.2 slice.2362
  649.9 0.2 slice.2363
  656.5 0.8 bitcast_dynamic-update-slice_fusion.2
  657.4 1.1 multiply_add_fusion.88
  659.4 0.2 slice.2362
  660.0 0.2 slice.2363
  666.5 0.8 bitcast_dynamic-update-slice_fusion.2
  667.3 19.4 %all_to_all.32 = bf16[8,256,256]{2,1,0:T(8,128)(2,1)S(1)} all-to-all(bf16[8,256,256]{2,1,0:T(8,128)(2,1)} %get-tuple-element.142), channel_id=1, replica_groups=mesh['stn'=64,'tm'=8] {'tm'}, dimensions={0} | all-to-all | bytes 2097152 | tf_op jit(solution)/shard_map/all_to_all | solution.py:114
  686.7 1.1 copy.10
  (2727 shorter events, 46.4 us)
Async XLA Ops:
  6.5 266.1 %all-reduce.100.cloned.1.call-start = ((), (), s32[]{:S(2)}) async-start(), calls=%async_computation.2 | async-start | bytes 524288 | tf_op jit(solution)/shard_map/psum | solution.py:9
  9.3 531.4 %all-reduce.102.cloned.1.call-start = ((), (), s32[]{:S(2)}) async-start(), calls=%async_computation.3 | async-start | bytes 524288 | tf_op jit(solution)/shard_map/psum | solution.py:9
  274.4 4.1 copy-start
  545.7 15.1 %copy-start.1 = (s32[2048]{0:T(1024)S(1)}, s32[2048]{0:T(1024)}, u32[]{:S(2)}) copy-start(s32[2048]{0:T(1024)} %param.13) | copy-start | bytes 24580
  545.7 41.4 %all-to-all-start = ((f32[256,8,256]{2,0,1:T(8,128)}), f32[256,8,256]{2,0,1:T(8,128)}, u32[]{:S(2)}, u32[]{:S(2)}) async-start(f32[256,8,256]{2,0,1:T(8,128)} %bitcast.38), calls=%async_computation | async-start | bytes 4194304 | tf_op jit(solution)/shard_map/all_to_all | solution.py:99
Sparse Core Ops, SparseCore 0:
  10.8 261.8 all-reduce.99
  279.8 260.8 all-reduce.101
where the time goes:
time: 695 us
  waiting for transfers between devices  547 us (79%)
  local copies, waits for them, and re-layouts  42 us (6%)
  other arithmetic  31.4 us (5%)
  blocking collectives  19.4 us (3%)
  starting transfers between devices  15.1 us (2%)
  loops' own time  14.9 us (2%)
  between operations  14.2 us (2%)
  matrix products  10.7 us (2%)
    psum x2, waiting for transfers between devices, broadcast(): return lax.psum(block, axis)  521 us
    slice x1216, local copies, waits for them, and re-layouts, block_prefix(): return lax.associative_scan(compose, elements, axis=0)  29.4 us
    all_to_all x1, waiting for transfers between devices, on_device(): series = lax.all_to_all(work, 'tm', split_axis=1, concat_axis=0, tiled=True)  25.5 us
    all_to_all x1, blocking collectives, on_device(): return lax.all_to_all(levels, 'tm', split_axis=0, concat_axis=1, tiled=True)  19.4 us
    all_to_all x1, starting transfers between devices, on_device(): series = lax.all_to_all(work, 'tm', split_axis=1, concat_axis=0, tiled=True)  15.1 us
    another operation x1, loops' own time, on_device(): lax.scan(advance, (zeros_row, zeros_row), (series_blocks, gap_blocks))  14.9 us
  transfers between devices with their start and end apart: 3, of which 3 were waited for; matrix products, arithmetic and copies ran while one was open for 1% of the time, Pallas kernels for 0%

commit v1 on v0

--- a/solution.py
+++ b/solution.py
@@ -6,7 +6,7 @@
 
 def broadcast(block, axis, source):
     block = jnp.where(lax.axis_index(axis) == source, block, jnp.zeros_like(block))
-    return lax.psum(block, axis)
+    return jnp.sum(lax.all_gather(block, axis), axis=0)
 
 
 def compose(earlier, later):

time: 695 us -> 580 us (0.83)
  waiting for transfers between devices: 547 us -> 410 us
  other arithmetic: 31.4 us -> 50.6 us
  local copies, waits for them, and re-layouts: 42 us -> 53.2 us
  starting transfers between devices: 15.1 us -> 5.86 us
    psum x2 -> x0, waiting for transfers between devices: 521 us -> none  [broadcast(): return lax.psum(block, axis)]
    all_gather x0 -> x2, waiting for transfers between devices: none -> 385 us  [broadcast(): return jnp.sum(lax.all_gather(block, axis), axis=0)]
    reduce_sum x0 -> x2, other arithmetic: none -> 13.7 us  [broadcast(): return jnp.sum(lax.all_gather(block, axis), axis=0)]
    while x32, local copies, waits for them, and re-layouts: 0.88 us -> 12.1 us
    all_to_all x1, starting transfers between devices: 15.1 us -> 5.82 us  [on_device(): series = lax.all_to_all(work, 'tm', split_axis=1, concat_axis=0, tiled=True)]
where the time goes in v1:
time: 580 us; the launch traced here: 579 us
  waiting for transfers between devices  410 us (71%)
  local copies, waits for them, and re-layouts  53.2 us (9%)
  other arithmetic  50.6 us (9%)
  blocking collectives  19.4 us (3%)
  loops' own time  14.7 us (3%)
  between operations  14.1 us (2%)
  matrix products  10.6 us (2%)
  starting transfers between devices  5.86 us (1%)
    all_gather x2, waiting for transfers between devices, broadcast(): return jnp.sum(lax.all_gather(block, axis), axis=0)  385 us
    slice x1216, local copies, waits for them, and re-layouts, block_prefix(): return lax.associative_scan(compose, elements, axis=0)  29.4 us
    all_to_all x1, waiting for transfers between devices, on_device(): series = lax.all_to_all(work, 'tm', split_axis=1, concat_axis=0, tiled=True)  25.5 us
    all_to_all x1, blocking collectives, on_device(): return lax.all_to_all(levels, 'tm', split_axis=0, concat_axis=1, tiled=True)  19.4 us
    another operation x1, loops' own time, on_device(): lax.scan(advance, (zeros_row, zeros_row), (series_blocks, gap_blocks))  14.7 us
    reduce_sum x2, other arithmetic, broadcast(): return jnp.sum(lax.all_gather(block, axis), axis=0)  13.7 us
    while x32, local copies, waits for them, and re-layouts  12.1 us
  transfers between devices with their start and end apart: 3, of which 3 were waited for; matrix products, arithmetic and copies ran while one was open for 1% of the time, Pallas kernels for 0%

profile of v1, /device:TPU:1, one launch (start us, length us, event | category | flops | bytes accessed | tf_op | source)
XLA Modules:
  0.0 578.8 jit_solution(1645186814230150447)
XLA Ops:
  7.2 2.1 convolution_select_fusion.1
  9.4 2.8 convert_element_type.29
  12.2 195.5 %all-gather.5.cloned.1.call-done = f32[16384,256]{1,0:T(8,128)} async-done(((f32[256,256]{1,0:T(8,128)}), f32[16384,256]{1,0:T(8,128)}) %all-gather.5.cloned.1.call-update) | async-done | bytes 16777232 | tf_op jit(solution)/shard_map/all_gather | solution.py:9
  207.7 6.8 %reduce_sum.18 = f32[256,256]{1,0:T(8,128)S(1)} reduce(f32[64,256,256]{2,1,0:T(8,128)} %bitcast.57, f32[]{:T(128)} %constant.83.clone.1), dimensions={0}, to_apply=%region_0.1 | reduce | flops 4128768 | bytes 17039364 | tf_op jit(solution)/shard_map/reduce_sum | solution.py:9
  214.5 1.7 select_dynamic-update-slice_fusion.1
  216.3 4.0 convolution_subtract_fusion.1
  220.3 1.1 convolution_select_fusion
  221.5 189.4 %all-gather.7.cloned.1.call-done = f32[16384,256]{1,0:T(8,128)} async-done(((f32[256,256]{1,0:T(8,128)}), f32[16384,256]{1,0:T(8,128)}) %all-gather.7.cloned.1.call-update) | async-done | bytes 16777232 | tf_op jit(solution)/shard_map/all_gather | solution.py:9
  410.8 6.8 %reduce_sum.19 = f32[256,256]{1,0:T(8,128)S(1)} reduce(f32[64,256,256]{2,1,0:T(8,128)} %bitcast.58, f32[]{:T(128)} %constant.83.clone.1), dimensions={0}, to_apply=%region_1.2 | reduce | flops 4128768 | bytes 17039364 | tf_op jit(solution)/shard_map/reduce_sum | solution.py:9
  417.7 3.4 convolution_subtract_fusion
  421.1 1.5 copy.12
  422.6 5.8 %all-to-all-start = ((f32[256,8,256]{2,0,1:T(8,128)}), f32[256,8,256]{2,0,1:T(8,128)}, u32[]{:S(2)}, u32[]{:S(2)}) async-start(f32[256,8,256]{2,0,1:T(8,128)} %bitcast.40), calls=%async_computation | async-start | bytes 4194304 | tf_op jit(solution)/shard_map/all_to_all | solution.py:99
  428.4 0.8 fusion.26
  429.2 25.5 %all-to-all-done = f32[256,8,256]{2,0,1:T(8,128)} async-done(((f32[256,8,256]{2,0,1:T(8,128)}), f32[256,8,256]{2,0,1:T(8,128)}, u32[]{:S(2)}, u32[]{:S(2)}) %all-to-all-start) | async-done | bytes 2097184 | tf_op jit(solution)/shard_map/all_to_all | solution.py:99
  454.7 96.8 %while.17 = (s32[]{:T(128)}, f32[256]{0:T(256)S(1)}, f32[256]{0:T(256)S(1)}, bf16[8,256,256]{2,1,0:T(8,128)(2,1)}, s32[8,256]{1,0:T(8,128)S(1)}, /*index=5*/f32[...) while((s32[]{:T(128)}, f32[256]{0:T(256)S(1)}, ...), condition=%wide.region_3.4_spmd, body=%wide.region_2.3_spmd.sunk | while | flops 4393474 | bytes 37128132 | solution.py:112
  454.8 1.1 multiply_add_fusion.88
  462.6 1.4 pad.1195
  465.3 0.8 bitcast_dynamic-update-slice_fusion.2
  466.1 0.7 add_add_fusion.38
  466.9 1.1 multiply_add_fusion.88
  474.7 1.4 pad.1195
  477.4 0.8 bitcast_dynamic-update-slice_fusion.2
  478.2 0.7 add_add_fusion.38
  479.0 1.1 multiply_add_fusion.88
  486.8 1.4 pad.1195
  489.5 0.8 bitcast_dynamic-update-slice_fusion.2
  490.3 0.7 add_add_fusion.38
  491.1 1.1 multiply_add_fusion.88
  498.9 1.4 pad.1195
  501.6 0.8 bitcast_dynamic-update-slice_fusion.2
  502.4 0.7 add_add_fusion.38
  503.2 1.1 multiply_add_fusion.88
  511.0 1.4 pad.1195
  513.7 0.8 bitcast_dynamic-update-slice_fusion.2
  514.5 0.7 add_add_fusion.38
  515.3 1.1 multiply_add_fusion.88
  523.1 1.4 pad.1195
  525.8 0.8 bitcast_dynamic-update-slice_fusion.2
  526.6 0.7 add_add_fusion.38
  527.4 1.1 multiply_add_fusion.88
  535.2 1.4 pad.1195
  537.9 0.8 bitcast_dynamic-update-slice_fusion.2
  538.7 0.7 add_add_fusion.38
  539.5 1.1 multiply_add_fusion.88
  547.3 1.4 pad.1195
  550.0 0.8 bitcast_dynamic-update-slice_fusion.2
  551.5 19.4 %all_to_all.32 = bf16[8,256,256]{2,1,0:T(8,128)(2,1)S(1)} all-to-all(bf16[8,256,256]{2,1,0:T(8,128)(2,1)} %get-tuple-element.142), channel_id=1, replica_groups=mesh['stn'=64,'tm'=8] {'tm'}, dimensions={0} | all-to-all | bytes 2097152 | tf_op jit(solution)/shard_map/all_to_all | solution.py:114
  570.9 1.1 copy.10
  (2729 shorter events, 50.6 us)
Async XLA Ops:
  6.5 201.1 %all-gather.5.cloned.1.call-start = ((), (), s32[]{:S(2)}) async-start(), calls=%async_computation.2 | async-start | bytes 17039360 | tf_op jit(solution)/shard_map/all_gather | solution.py:9
  9.3 401.5 %all-gather.7.cloned.1.call-start = ((), (), s32[]{:S(2)}) async-start(), calls=%async_computation.3 | async-start | bytes 17039360 | tf_op jit(solution)/shard_map/all_gather | solution.py:9
  216.3 4.0 copy-start
  422.6 5.8 %copy-start.1 = (s32[2048]{0:T(1024)S(1)}, s32[2048]{0:T(1024)}, u32[]{:S(2)}) copy-start(s32[2048]{0:T(1024)} %param.13) | copy-start | bytes 24580
  422.6 32.1 %all-to-all-start = ((f32[256,8,256]{2,0,1:T(8,128)}), f32[256,8,256]{2,0,1:T(8,128)}, u32[]{:S(2)}, u32[]{:S(2)}) async-start(f32[256,8,256]{2,0,1:T(8,128)} %bitcast.40), calls=%async_computation | async-start | bytes 4194304 | tf_op jit(solution)/shard_map/all_to_all | solution.py:99
Sparse Core Ops, SparseCore 0:
  10.3 197.3 all-gather.4
  221.6 189.2 all-gather.6
